TPU v7x, 32 devices: a whole 2x2x4 slice. The times are simulated.
32 devices in a mesh: row: 4 (over y, core), col: 8 (over z, x).
Axes of the slice: x: 2, y: 2, z: 4, core: 2. Of those that a mesh axis runs over, the one named last changes fastest.
Arguments:
- positions: float32 [3, 512], P(None, ('row', 'col')), as said below
- thermal_noise: float32 [32, 3, 512], P(None, None, ('row', 'col')), as said below
Outputs:
- displacement: float32 [32, 3, 512], P(None, None, ('row', 'col'))
Inputs may be any that keep to these rules, and one draw needn't show every extreme that they name: `positions`: any two particles are at least 1.0 apart. `thermal_noise`: finite real entries.
All inputs are finite; a program needn't handle non-finite values.
Results may differ from a plain program's by a relative error of at most 0.0013.
Values may be sent and summed in bfloat16 or wider, within the bound.
A program may use at most 64 MiB of HBM per device.

v0:
```python
import jax
import jax.numpy as jnp
from jax import lax
from jax.sharding import PartitionSpec as P


def pair_tensor(rows_pos, cols_pos, retain):
    offsets = [rows_pos[a][None, :] - cols_pos[a][:, None] for a in range(3)]
    squared = offsets[0] * offsets[0] + offsets[1] * offsets[1] + offsets[2] * offsets[2]
    guarded = jnp.where(retain, squared, 4.0)
    inverse = lax.rsqrt(guarded)
    distance = guarded * inverse
    correlation = distance < 2.0
    inverse_cube = inverse * inverse * inverse
    inverse_fifth = inverse_cube * inverse * inverse
    isotropic = jnp.where(
        correlation, 1.0 - 0.28125 * distance, 0.75 * inverse + 0.5 * inverse_cube
    )
    dyadic = jnp.where(correlation, 0.09375 * inverse, 0.75 * inverse_cube - 1.5 * inverse_fifth)
    isotropic = jnp.where(retain, isotropic, 0.0)
    dyadic = jnp.where(retain, dyadic, 0.0)
    columns = []
    for b in range(3):
        elements = []
        for a in range(3):
            element = dyadic * offsets[a] * offsets[b]
            if a == b:
                element = element + isotropic
            elements.append(element)
        columns.append(jnp.stack(elements, axis=1))
    return jnp.stack(columns, axis=0)


def half_image(pos_rows, pos_cols, vec_rows, vec_cols, own_vector):
    row_devices = lax.axis_size("row")
    col_devices = lax.axis_size("col")
    row_index = lax.axis_index("row")
    col_index = lax.axis_index("col")
    samples = own_vector.shape[0]
    per_device = own_vector.shape[2]
    row_count = pos_rows.shape[1]
    row_label = row_index * col_devices * per_device + lax.iota(jnp.int32, row_count)
    group_size = min(row_devices, max(1, 128 // per_device))
    width = group_size * per_device
    group_count = row_devices // group_size
    sum_rows = jnp.zeros((samples, 3, row_count), jnp.float32)
    sum_cols = jnp.zeros((samples, 3, per_device * row_devices), jnp.float32)

    def add_group(group, totals):
        sum_rows, sum_cols = totals
        start = group * width
        cols_pos = lax.dynamic_slice_in_dim(pos_cols, start, width, 1)
        cols_vec = lax.dynamic_slice_in_dim(vec_cols, start, width, 2)
        local_cols = lax.iota(jnp.int32, width)
        segment = group * group_size + local_cols // per_device
        col_label = (segment * col_devices + col_index) * per_device + local_cols % per_device
        keep = segment >= row_index
        upper = (segment != row_index)[:, None] | (row_label[None, :] < col_label[:, None])
        retain = keep[:, None] & upper & (row_label[None, :] != col_label[:, None])
        tensor = pair_tensor(pos_rows, cols_pos, retain).astype(jnp.bfloat16)
        sum_rows = sum_rows + jnp.einsum(
            "kbj,bjai->kai", cols_vec, tensor, preferred_element_type=jnp.float32
        )
        credit = jnp.einsum("kai,bjai->kbj", vec_rows, tensor, preferred_element_type=jnp.float32)
        previous = lax.dynamic_slice_in_dim(sum_cols, start, width, 2)
        sum_cols = lax.dynamic_update_slice_in_dim(sum_cols, previous + credit, start, 2)
        return (sum_rows, sum_cols)

    totals = (sum_rows, sum_cols)
    totals = lax.fori_loop(row_index // group_size, group_count, add_group, totals)
    sum_rows, sum_cols = totals
    mobility_image = own_vector + lax.psum_scatter(sum_rows, "col", scatter_dimension=2, tiled=True)
    return mobility_image + lax.psum_scatter(sum_cols, "row", scatter_dimension=2, tiled=True)


def on_device(positions, thermal_noise):
    squares = lax.psum(jnp.sum(thermal_noise * thermal_noise, axis=(1, 2)), ("row", "col"))
    noise_length = jnp.sqrt(squares + 1e-06)
    basis_one = thermal_noise / noise_length[:, None, None]
    pos_cols, cols_one = (
        lax.all_gather(positions, "row", axis=1, tiled=True),
        lax.all_gather(basis_one, "row", axis=2, tiled=True),
    )
    pos_rows, rows_wide = (
        lax.all_gather(positions, "col", axis=1, tiled=True),
        lax.all_gather(basis_one, "col", axis=2, tiled=True),
    )
    image_one = half_image(
        pos_rows, pos_cols, rows_wide.astype(jnp.bfloat16), cols_one.astype(jnp.bfloat16), basis_one
    )
    alpha_one = lax.psum(jnp.sum(basis_one * image_one, axis=(1, 2)), ("row", "col"))
    remainder = image_one - alpha_one[:, None, None] * basis_one
    beta_squared = lax.psum(jnp.sum(remainder * remainder, axis=(1, 2)), ("row", "col"))
    beta_one = jnp.sqrt(beta_squared + 1e-06)
    basis_two = remainder / beta_one[:, None, None]
    narrow_two = basis_two.astype(jnp.bfloat16)
    cols_two = lax.all_gather(narrow_two, "row", axis=2, tiled=True)
    rows_two = lax.all_gather(narrow_two, "col", axis=2, tiled=True)
    image_two = half_image(pos_rows, pos_cols, rows_two, cols_two, basis_two)
    alpha_two = lax.psum(jnp.sum(basis_two * image_two, axis=(1, 2)), ("row", "col"))
    det_root = jnp.sqrt(alpha_one * alpha_two - beta_one * beta_one)
    trace_root = jnp.sqrt(alpha_one + alpha_two + 2.0 * det_root)
    weight_one = (alpha_one + det_root) / trace_root
    weight_two = beta_one / trace_root
    return (
        0.5
        * noise_length[:, None, None]
        * (weight_one[:, None, None] * basis_one + weight_two[:, None, None] * basis_two)
    )


def solution(mesh):
    return jax.shard_map(
        on_device,
        mesh=mesh,
        in_specs=(P(None, ("row", "col")), P(None, None, ("row", "col"))),
        out_specs=P(None, None, ("row", "col")),
        check_vma=False,
    )
```

profile of v0, /device:TPU:0, one launch (start us, length us, event | category | flops | bytes accessed | tf_op | source)
XLA Modules:
  0.0 451.7 jit_solution(3374881495807771110)
XLA Ops:
  6.5 0.7 copy-done.3
  7.2 28.1 %all-gather = f32[8,16,3]{1,2,0:T(4,128)S(1)} all-gather(f32[1,16,3]{1,2,0:T(4,128)S(1)} %bitcast.133), channel_id=1, replica_groups=mesh['row'=4,'col'=8] {'col'}, dimensions={0}, use_global_device_ids=true | all-gather | bytes 1728 | tf_op jit(solution)/shard_map/all_gather | solution.py:85
  35.3 5.2 %all-gather.1 = f32[4,16,3]{1,2,0:T(4,128)S(1)} all-gather(f32[1,16,3]{1,2,0:T(4,128)S(1)} %bitcast.134), channel_id=1, replica_groups=mesh['row'=4,'col'=8] {'row'}, dimensions={0}, use_global_device_ids=true | all-gather | bytes 960 | tf_op jit(solution)/shard_map/all_gather | solution.py:81
  40.5 38.9 %psum.28 = f32[32]{0:T(128)S(1)} all-reduce(f32[32]{0:T(128)S(1)} %multiply_reduce_fusion.3), channel_id=1, replica_groups=mesh['row'=4,'col'=8] {'row','col'}, use_global_device_ids=true, to_apply=%region_1.0 | all-reduce | flops 32 | bytes 256 | tf_op jit(solution)/shard_map/psum | solution.py:77
  79.5 5.5 %all_gather.20 = bf16[32,3,64]{0,2,1:T(8,128)(2,1)S(1)} all-gather(bf16[32,3,16]{0,2,1:T(8,128)(2,1)S(1)} %convert.110), channel_id=1, replica_groups=mesh['row'=4,'col'=8] {'row'}, dimensions={2}, use_global_device_ids=true | all-gather | bytes 15360 | tf_op jit(solution)/shard_map/all_gather | solution.py:82
  85.1 30.6 %all_gather.21 = bf16[32,3,128]{0,2,1:T(8,128)(2,1)S(1)} all-gather(bf16[32,3,16]{0,2,1:T(8,128)(2,1)S(1)} %get-tuple-element.415), channel_id=1, replica_groups=mesh['row'=4,'col'=8] {'col'}, dimensions={2}, use_global_device_ids=true | all-gather | bytes 27648 | tf_op jit(solution)/shard_map/all_gather | solution.py:86
  115.9 0.7 while.30
  116.6 0.7 copy.42
  117.5 0.8 copy.41
  118.3 17.6 %reduce-scatter.7.cloned.1.call-done = f32[32,3,16]{0,2,1:T(8,128)} async-done(((f32[32,3,64]{0,2,1:T(8,128)}), f32[32,3,16]{0,2,1:T(8,128)}) %reduce-scatter.7.cloned.1.call-update) | async-done | bytes 6160 | tf_op jit(solution)/shard_map/reduce_scatter | solution.py:73
  135.9 65.3 %reduce-scatter.5.cloned.1.call-done = f32[32,3,16]{0,2,1:T(8,128)} async-done(((f32[32,3,128]{0,2,1:T(8,128)}), f32[32,3,16]{0,2,1:T(8,128)}) %reduce-scatter.5.cloned.1.call-update) | async-done | bytes 6160 | tf_op jit(solution)/shard_map/reduce_scatter | solution.py:72
  201.2 0.8 multiply_reduce_fusion.2
  202.1 40.1 %psum.29 = f32[32]{0:T(128)S(1)} all-reduce(f32[32]{0:T(128)S(1)} %multiply_reduce_fusion.2), channel_id=1, replica_groups=mesh['row'=4,'col'=8] {'row','col'}, use_global_device_ids=true, to_apply=%region_7.8 | all-reduce | flops 32 | bytes 256 | tf_op jit(solution)/shard_map/psum | solution.py:91
  242.2 39.1 %psum.30 = f32[32]{0:T(128)S(1)} all-reduce(f32[32]{0:T(128)S(1)} %get-tuple-element.413), channel_id=1, replica_groups=mesh['row'=4,'col'=8] {'row','col'}, use_global_device_ids=true, to_apply=%region_9.10 | all-reduce | flops 32 | bytes 256 | tf_op jit(solution)/shard_map/psum | solution.py:93
  281.3 30.5 %all_gather.23 = bf16[32,3,128]{0,2,1:T(8,128)(2,1)S(1)} all-gather(bf16[32,3,16]{0,2,1:T(8,128)(2,1)S(1)} %fusion.71), channel_id=1, replica_groups=mesh['row'=4,'col'=8] {'col'}, dimensions={2}, use_global_device_ids=true | all-gather | bytes 27648 | tf_op jit(solution)/shard_map/all_gather | solution.py:98
  311.9 5.5 %all_gather.22 = bf16[32,3,64]{0,2,1:T(8,128)(2,1)S(1)} all-gather(bf16[32,3,16]{0,2,1:T(8,128)(2,1)S(1)} %fusion.71), channel_id=1, replica_groups=mesh['row'=4,'col'=8] {'row'}, dimensions={2}, use_global_device_ids=true | all-gather | bytes 15360 | tf_op jit(solution)/shard_map/all_gather | solution.py:97
  317.6 0.7 while.31
  318.4 0.7 copy.46
  319.2 0.8 copy.45
  320.0 18.4 %reduce-scatter.11.cloned.1.call-done = f32[32,3,16]{0,2,1:T(8,128)} async-done(((f32[32,3,64]{0,2,1:T(8,128)}), f32[32,3,16]{0,2,1:T(8,128)}) %reduce-scatter.11.cloned.1.call-update) | async-done | bytes 6160 | tf_op jit(solution)/shard_map/reduce_scatter | solution.py:73
  338.4 65.2 %reduce-scatter.9.cloned.1.call-done = f32[32,3,16]{0,2,1:T(8,128)} async-done(((f32[32,3,128]{0,2,1:T(8,128)}), f32[32,3,16]{0,2,1:T(8,128)}) %reduce-scatter.9.cloned.1.call-update) | async-done | bytes 6160 | tf_op jit(solution)/shard_map/reduce_scatter | solution.py:72
  403.6 0.8 multiply_reduce_fusion
  404.4 40.2 %psum.31 = f32[32]{0:T(128)S(1)} all-reduce(f32[32]{0:T(128)S(1)} %multiply_reduce_fusion), channel_id=1, replica_groups=mesh['row'=4,'col'=8] {'row','col'}, use_global_device_ids=true, to_apply=%region_15.16 | all-reduce | flops 32 | bytes 256 | tf_op jit(solution)/shard_map/psum | solution.py:100
  444.6 0.6 add_multiply_fusion
  (57 shorter events, 2.1 us)
Async XLA Ops:
  6.5 129.4 %reduce-scatter.7.cloned.1.call-start = ((), (), s32[]{:S(2)}) async-start(), calls=%async_computation.5 | async-start | bytes 122880 | tf_op jit(solution)/shard_map/reduce_scatter | solution.py:73
  6.5 0.7 copy-start.3
  7.2 33.2 %copy-start = (f32[32,3,16]{0,2,1:T(8,128)S(1)}, f32[32,3,16]{0,2,1:T(8,128)}, u32[]{:S(2)}) copy-start(f32[32,3,16]{0,2,1:T(8,128)} %param.7) | copy-start | bytes 18436
  117.4 83.8 %reduce-scatter.5.cloned.1.call-start = ((), (), s32[]{:S(2)}) async-start(), calls=%async_computation.4 | async-start | bytes 221184 | tf_op jit(solution)/shard_map/reduce_scatter | solution.py:72
  118.3 220.2 %reduce-scatter.11.cloned.1.call-start = ((), (), s32[]{:S(2)}) async-start(), calls=%async_computation.7 | async-start | bytes 122880 | tf_op jit(solution)/shard_map/reduce_scatter | solution.py:73
  135.9 106.2 %copy-start.1 = (f32[32,3,16]{0,2,1:T(8,128)S(1)}, f32[32,3,16]{0,2,1:T(8,128)}, u32[]{:S(2)}) copy-start(f32[32,3,16]{0,2,1:T(8,128)} %reduce-scatter.7.cloned.1.call-done) | copy-start | bytes 18436
  201.2 40.9 %copy-start.2 = (f32[32,3,16]{0,2,1:T(8,128)S(1)}, f32[32,3,16]{0,2,1:T(8,128)}, u32[]{:S(2)}) copy-start(f32[32,3,16]{0,2,1:T(8,128)} %reduce-scatter.5.cloned.1.call-done) | copy-start | bytes 18436
  319.1 84.5 %reduce-scatter.9.cloned.1.call-start = ((), (), s32[]{:S(2)}) async-start(), calls=%async_computation.6 | async-start | bytes 221184 | tf_op jit(solution)/shard_map/reduce_scatter | solution.py:72
Sparse Core Ops, SparseCore 0:
  117.5 18.3 reduce-scatter.6
  139.2 61.9 reduce-scatter.4
  319.2 19.1 reduce-scatter.10
  341.6 61.9 reduce-scatter.8
where the time goes:
time: 453 us; the launch traced here: 452 us
  blocking collectives  264 us (58%)
  waiting for transfers between devices  167 us (37%)
  between operations  13.2 us (3%)
    reduce_scatter x2, waiting for transfers between devices, half_image(): lax.psum_scatter(sum_rows, 'col', scatter_dimension=2, tiled=True)  130 us
    psum x1, blocking collectives, on_device(): lax.psum(jnp.sum(basis_two * image_two, axis=(1, 2)), ('row', 'col'))  40.2 us
    psum x1, blocking collectives, on_device(): lax.psum(jnp.sum(basis_one * image_one, axis=(1, 2)), ('row', 'col'))  40.1 us
    psum x1, blocking collectives, on_device(): lax.psum(jnp.sum(remainder * remainder, axis=(1, 2)), ('row', 'col'))  39.1 us
    psum x1, blocking collectives, on_device(): lax.psum(jnp.sum(thermal_noise * thermal_noise, axis=(1, 2)), ('row', 'co...  38.9 us
    reduce_scatter x2, waiting for transfers between devices, half_image(): lax.psum_scatter(sum_cols, 'row', scatter_dimension=2, tiled=True)  36 us
    all_gather x1, blocking collectives, on_device(): lax.all_gather(basis_one, 'col', axis=2, tiled=True)  30.6 us
    all_gather x1, blocking collectives, on_device(): rows_two = lax.all_gather(narrow_two, 'col', axis=2, tiled=True)  30.5 us
  transfers between devices with their start and end apart: 4, of which 4 were waited for; matrix products, arithmetic and copies ran while one was open for 0% of the time, Pallas kernels for 0%

commit v1 on v0

--- a/solution.py
+++ b/solution.py
@@ -97,7 +97,9 @@
     cols_two = lax.all_gather(narrow_two, "row", axis=2, tiled=True)
     rows_two = lax.all_gather(narrow_two, "col", axis=2, tiled=True)
     image_two = half_image(pos_rows, pos_cols, rows_two, cols_two, basis_two)
-    alpha_two = lax.psum(jnp.sum(basis_two * image_two, axis=(1, 2)), ("row", "col"))
+    alpha_two = jax.lax.psum(
+        jax.lax.psum(jnp.sum(basis_two * image_two, axis=(1, 2)), "col"), "row"
+    )
     det_root = jnp.sqrt(alpha_one * alpha_two - beta_one * beta_one)
     trace_root = jnp.sqrt(alpha_one + alpha_two + 2.0 * det_root)
     weight_one = (alpha_one + det_root) / trace_root

time: 453 us -> 437 us (0.965)
  blocking collectives: 264 us -> 249 us
    psum x1 -> x2, blocking collectives: 40.2 us -> 25.1 us  [the longest x1 19.5 us: on_device(): jax.lax.psum(jnp.sum(basis_two * image_two, axis=(1, 2)), 'col')]
where the time goes in v1:
time: 437 us
  blocking collectives  249 us (57%)
  waiting for transfers between devices  167 us (38%)
  between operations  13.2 us (3%)
    reduce_scatter x2, waiting for transfers between devices, half_image(): lax.psum_scatter(sum_rows, 'col', scatter_dimension=2, tiled=True)  130 us
    psum x1, blocking collectives, on_device(): lax.psum(jnp.sum(basis_one * image_one, axis=(1, 2)), ('row', 'col'))  40.1 us
    psum x1, blocking collectives, on_device(): lax.psum(jnp.sum(remainder * remainder, axis=(1, 2)), ('row', 'col'))  39.1 us
    psum x1, blocking collectives, on_device(): lax.psum(jnp.sum(thermal_noise * thermal_noise, axis=(1, 2)), ('row', 'co...  38.9 us
    reduce_scatter x2, waiting for transfers between devices, half_image(): lax.psum_scatter(sum_cols, 'row', scatter_dimension=2, tiled=True)  36 us
    all_gather x1, blocking collectives, on_device(): lax.all_gather(basis_one, 'col', axis=2, tiled=True)  30.6 us
    all_gather x1, blocking collectives, on_device(): rows_two = lax.all_gather(narrow_two, 'col', axis=2, tiled=True)  30.5 us
    all_gather x1, blocking collectives, on_device(): lax.all_gather(positions, 'col', axis=1, tiled=True)  28.1 us
  transfers between devices with their start and end apart: 4, of which 4 were waited for; matrix products, arithmetic and copies ran while one was open for 0% of the time, Pallas kernels for 0%

profile of v1, /device:TPU:0, one launch (start us, length us, event | category | flops | bytes accessed | tf_op | source)
XLA Modules:
  0.0 436.7 jit_solution(14192137315507088966)
XLA Ops:
  6.5 0.7 copy-done.3
  7.2 28.1 %all-gather = f32[8,16,3]{1,2,0:T(4,128)S(1)} all-gather(f32[1,16,3]{1,2,0:T(4,128)S(1)} %bitcast.133), channel_id=1, replica_groups=mesh['row'=4,'col'=8] {'col'}, dimensions={0}, use_global_device_ids=true | all-gather | bytes 1728 | tf_op jit(solution)/shard_map/all_gather | solution.py:85
  35.3 5.2 %all-gather.1 = f32[4,16,3]{1,2,0:T(4,128)S(1)} all-gather(f32[1,16,3]{1,2,0:T(4,128)S(1)} %bitcast.134), channel_id=1, replica_groups=mesh['row'=4,'col'=8] {'row'}, dimensions={0}, use_global_device_ids=true | all-gather | bytes 960 | tf_op jit(solution)/shard_map/all_gather | solution.py:81
  40.5 38.9 %psum.35 = f32[32]{0:T(128)S(1)} all-reduce(f32[32]{0:T(128)S(1)} %multiply_reduce_fusion.3), channel_id=1, replica_groups=mesh['row'=4,'col'=8] {'row','col'}, use_global_device_ids=true, to_apply=%region_1.0 | all-reduce | flops 32 | bytes 256 | tf_op jit(solution)/shard_map/psum | solution.py:77
  79.5 5.5 %all_gather.20 = bf16[32,3,64]{0,2,1:T(8,128)(2,1)S(1)} all-gather(bf16[32,3,16]{0,2,1:T(8,128)(2,1)S(1)} %convert.110), channel_id=1, replica_groups=mesh['row'=4,'col'=8] {'row'}, dimensions={2}, use_global_device_ids=true | all-gather | bytes 15360 | tf_op jit(solution)/shard_map/all_gather | solution.py:82
  85.1 30.6 %all_gather.21 = bf16[32,3,128]{0,2,1:T(8,128)(2,1)S(1)} all-gather(bf16[32,3,16]{0,2,1:T(8,128)(2,1)S(1)} %get-tuple-element.415), channel_id=1, replica_groups=mesh['row'=4,'col'=8] {'col'}, dimensions={2}, use_global_device_ids=true | all-gather | bytes 27648 | tf_op jit(solution)/shard_map/all_gather | solution.py:86
  115.9 0.7 while.30
  116.6 0.7 copy.42
  117.5 0.8 copy.41
  118.3 17.6 %reduce-scatter.7.cloned.1.call-done = f32[32,3,16]{0,2,1:T(8,128)} async-done(((f32[32,3,64]{0,2,1:T(8,128)}), f32[32,3,16]{0,2,1:T(8,128)}) %reduce-scatter.7.cloned.1.call-update) | async-done | bytes 6160 | tf_op jit(solution)/shard_map/reduce_scatter | solution.py:73
  135.9 65.3 %reduce-scatter.5.cloned.1.call-done = f32[32,3,16]{0,2,1:T(8,128)} async-done(((f32[32,3,128]{0,2,1:T(8,128)}), f32[32,3,16]{0,2,1:T(8,128)}) %reduce-scatter.5.cloned.1.call-update) | async-done | bytes 6160 | tf_op jit(solution)/shard_map/reduce_scatter | solution.py:72
  201.2 0.8 multiply_reduce_fusion.2
  202.1 40.1 %psum.36 = f32[32]{0:T(128)S(1)} all-reduce(f32[32]{0:T(128)S(1)} %multiply_reduce_fusion.2), channel_id=1, replica_groups=mesh['row'=4,'col'=8] {'row','col'}, use_global_device_ids=true, to_apply=%region_7.8 | all-reduce | flops 32 | bytes 256 | tf_op jit(solution)/shard_map/psum | solution.py:91
  242.2 39.1 %psum.37 = f32[32]{0:T(128)S(1)} all-reduce(f32[32]{0:T(128)S(1)} %get-tuple-element.413), channel_id=1, replica_groups=mesh['row'=4,'col'=8] {'row','col'}, use_global_device_ids=true, to_apply=%region_9.10 | all-reduce | flops 32 | bytes 256 | tf_op jit(solution)/shard_map/psum | solution.py:93
  281.3 30.5 %all_gather.23 = bf16[32,3,128]{0,2,1:T(8,128)(2,1)S(1)} all-gather(bf16[32,3,16]{0,2,1:T(8,128)(2,1)S(1)} %fusion.71), channel_id=1, replica_groups=mesh['row'=4,'col'=8] {'col'}, dimensions={2}, use_global_device_ids=true | all-gather | bytes 27648 | tf_op jit(solution)/shard_map/all_gather | solution.py:98
  311.9 5.5 %all_gather.22 = bf16[32,3,64]{0,2,1:T(8,128)(2,1)S(1)} all-gather(bf16[32,3,16]{0,2,1:T(8,128)(2,1)S(1)} %fusion.71), channel_id=1, replica_groups=mesh['row'=4,'col'=8] {'row'}, dimensions={2}, use_global_device_ids=true | all-gather | bytes 15360 | tf_op jit(solution)/shard_map/all_gather | solution.py:97
  317.6 0.7 while.31
  318.4 0.7 copy.46
  319.2 0.8 copy.45
  320.0 18.4 %reduce-scatter.11.cloned.1.call-done = f32[32,3,16]{0,2,1:T(8,128)} async-done(((f32[32,3,64]{0,2,1:T(8,128)}), f32[32,3,16]{0,2,1:T(8,128)}) %reduce-scatter.11.cloned.1.call-update) | async-done | bytes 6160 | tf_op jit(solution)/shard_map/reduce_scatter | solution.py:73
  338.4 65.2 %reduce-scatter.9.cloned.1.call-done = f32[32,3,16]{0,2,1:T(8,128)} async-done(((f32[32,3,128]{0,2,1:T(8,128)}), f32[32,3,16]{0,2,1:T(8,128)}) %reduce-scatter.9.cloned.1.call-update) | async-done | bytes 6160 | tf_op jit(solution)/shard_map/reduce_scatter | solution.py:72
  403.6 0.8 multiply_reduce_fusion
  404.4 19.5 %psum.38 = f32[32]{0:T(128)S(1)} all-reduce(f32[32]{0:T(128)S(1)} %multiply_reduce_fusion), channel_id=1, replica_groups=mesh['row'=4,'col'=8] {'col'}, use_global_device_ids=true, to_apply=%region_15.16 | all-reduce | flops 32 | bytes 256 | tf_op jit(solution)/shard_map/psum | solution.py:101
  423.8 5.6 %psum.39 = f32[32]{0:T(128)S(1)} all-reduce(f32[32]{0:T(128)S(1)} %psum.38), channel_id=1, replica_groups=mesh['row'=4,'col'=8] {'row'}, use_global_device_ids=true, to_apply=%region_16.17 | all-reduce | flops 32 | bytes 256 | tf_op jit(solution)/shard_map/psum | solution.py:100
  (58 shorter events, 2.8 us)
Async XLA Ops:
  6.5 129.4 %reduce-scatter.7.cloned.1.call-start = ((), (), s32[]{:S(2)}) async-start(), calls=%async_computation.5 | async-start | bytes 122880 | tf_op jit(solution)/shard_map/reduce_scatter | solution.py:73
  6.5 0.7 copy-start.3
  7.2 33.2 %copy-start = (f32[32,3,16]{0,2,1:T(8,128)S(1)}, f32[32,3,16]{0,2,1:T(8,128)}, u32[]{:S(2)}) copy-start(f32[32,3,16]{0,2,1:T(8,128)} %param.7) | copy-start | bytes 18436
  117.4 83.8 %reduce-scatter.5.cloned.1.call-start = ((), (), s32[]{:S(2)}) async-start(), calls=%async_computation.4 | async-start | bytes 221184 | tf_op jit(solution)/shard_map/reduce_scatter | solution.py:72
  118.3 220.2 %reduce-scatter.11.cloned.1.call-start = ((), (), s32[]{:S(2)}) async-start(), calls=%async_computation.7 | async-start | bytes 122880 | tf_op jit(solution)/shard_map/reduce_scatter | solution.py:73
  135.9 106.2 %copy-start.1 = (f32[32,3,16]{0,2,1:T(8,128)S(1)}, f32[32,3,16]{0,2,1:T(8,128)}, u32[]{:S(2)}) copy-start(f32[32,3,16]{0,2,1:T(8,128)} %reduce-scatter.7.cloned.1.call-done) | copy-start | bytes 18436
  201.2 40.9 %copy-start.2 = (f32[32,3,16]{0,2,1:T(8,128)S(1)}, f32[32,3,16]{0,2,1:T(8,128)}, u32[]{:S(2)}) copy-start(f32[32,3,16]{0,2,1:T(8,128)} %reduce-scatter.5.cloned.1.call-done) | copy-start | bytes 18436
  319.1 84.5 %reduce-scatter.9.cloned.1.call-start = ((), (), s32[]{:S(2)}) async-start(), calls=%async_computation.6 | async-start | bytes 221184 | tf_op jit(solution)/shard_map/reduce_scatter | solution.py:72
Sparse Core Ops, SparseCore 0:
  117.5 18.3 reduce-scatter.6
  139.2 61.9 reduce-scatter.4
  319.2 19.1 reduce-scatter.10
  341.6 61.9 reduce-scatter.8
